TPU v7x, 32 devices: a whole 2x2x4 slice. The times are simulated.
32 devices in a mesh: grp: 8 (over z, core), exp: 4 (over y, x).
Axes of the slice: x: 2, y: 2, z: 4, core: 2. Of those that a mesh axis runs over, the one named last changes fastest.
Arguments:
- sky: float32 [32, 6, 8, 512], P(('grp', 'exp')), may hold values from -6 to 6
- observed: bfloat16 [128, 6, 8, 512], P(('grp', 'exp')), may hold values from -6 to 6
- intersections: int32 [128, 4], P(('grp', 'exp')), may hold values from 0 to 7
- resample_index: int32 [128, 4], P(('grp', 'exp')), may hold values from 0 to 7
- psf_index: int32 [128], P(('grp', 'exp')), may hold values from 0 to 15
- resample_table: bfloat16 [8, 512, 512], replicated, may hold values from -0.25 to 0.25
- psf_weights: float32 [16, 8], replicated, may hold values from -5 to 5
- psf_basis: float32 [8, 41], replicated, may hold values from -0.3125 to 0.3125
Outputs:
- sky_out: float32 [32, 6, 8, 512], P(('grp', 'exp'))
- residual: float32 [128, 6, 8, 512], P(('grp', 'exp'))
Inputs may be any that keep to these rules, and one draw needn't show every extreme that they name: `intersections`: with G = 4: an entry v below G names tile v of the exposure's own group; an entry v of G or more names tile v - G of the next group along grp, cyclically.
All inputs are finite; a program needn't handle non-finite values.
Results may differ from a plain program's by a relative error of at most 0.019.
Values may be sent and summed in bfloat16 or wider, within the bound.
A program may use at most 128 MiB of HBM per device.

v0:
```python
import jax
import jax.numpy as jnp
from jax import lax
from jax.sharding import PartitionSpec as P

ITERS = 2
STEP = 0.05


def shifted(block, axis, distance):
    devices = range(lax.axis_size(axis))
    route = [((i - distance) % len(devices), i) for i in devices]
    return lax.ppermute(block, axis, route)


def conv_matrices(kernels, width, taps):
    half = (taps - 1) // 2
    count = kernels.shape[0]
    head = kernels[:, half::-1]
    tail = kernels[:, taps - 1 : half : -1]
    blank = jnp.zeros((count, 2 * width - 1 - taps), jnp.float32)
    pattern = jnp.concatenate([head, blank, tail], axis=1)
    tiled = jnp.broadcast_to(pattern[:, None, :], (count, width, 2 * width - 1)).reshape(
        count, width * (2 * width - 1)
    )
    tiled = tiled[:, : width * (2 * width - 2)].reshape(count, width, 2 * width - 2)[:, :, :width]
    return tiled.astype(jnp.bfloat16)


def fetch_window(sky_half):
    own_group = lax.all_gather(sky_half, "exp", axis=0, tiled=True)
    next_group = shifted(own_group, "grp", -1)
    return jnp.concatenate([own_group, next_group], axis=0)


def return_partials(grads, group_tiles):
    own_part = grads[:group_tiles]
    next_part = grads[group_tiles:]
    arrived = shifted(next_part.astype(jnp.bfloat16), "grp", 1).astype(next_part.dtype)
    return lax.psum_scatter(
        (own_part + arrived).astype(jnp.bfloat16), "exp", scatter_dimension=0, tiled=True
    ).astype(jnp.float32)


def shards(
    sky, observed, intersections, resample_index, psf_index, resample_table, psf_weights, psf_basis
):
    exposures_here, intersection_count = intersections.shape
    group_tiles = sky.shape[0] * lax.axis_size("exp")
    width = resample_table.shape[1]
    taps = psf_basis.shape[1]
    table_rows = psf_weights.shape[0]
    res_count = resample_table.shape[0]
    selector = (
        psf_index[:, None] == lax.broadcasted_iota(jnp.int32, (exposures_here, table_rows), 1)
    ).astype(jnp.float32)
    weights = jnp.sum(selector[:, :, None] * psf_weights[None, :, :], axis=1)
    kernels = jnp.sum(weights[:, :, None] * psf_basis[None, :, :], axis=1)
    conv = conv_matrices(kernels, width, taps)
    window_iota = lax.broadcasted_iota(
        jnp.int32, (exposures_here, intersection_count, 2 * group_tiles), 2
    )
    tile_onehot = intersections[:, :, None] == window_iota
    pick_tiles = tile_onehot.astype(jnp.bfloat16)
    onehots = tile_onehot.astype(jnp.float32)
    res_iota = lax.broadcasted_iota(jnp.int32, (exposures_here, intersection_count, res_count), 2)
    pick_res = (resample_index[:, :, None] == res_iota).astype(jnp.bfloat16)
    matrices = jnp.einsum(
        "ekn,nwv->ekwv", pick_res, resample_table, preferred_element_type=jnp.float32
    ).astype(jnp.bfloat16)
    sky_out = sky
    residual = jnp.zeros(observed.shape, jnp.float32)
    for step in range(ITERS):
        window = fetch_window(sky_out.astype(jnp.bfloat16))
        chosen = jnp.einsum(
            "ekt,tbrw->ekbrw", pick_tiles, window, preferred_element_type=jnp.float32
        ).astype(jnp.bfloat16)
        pre = jnp.zeros(observed.shape, jnp.float32)
        for k in range(intersection_count):
            pre = pre + jnp.einsum(
                "ebrw,ewv->ebrv", chosen[:, k], matrices[:, k], preferred_element_type=jnp.float32
            )
        model = jnp.einsum(
            "ebrw,ewv->ebrv", pre.astype(jnp.bfloat16), conv, preferred_element_type=jnp.float32
        )
        residual = observed.astype(jnp.float32) - model
        back = jnp.einsum(
            "ebrv,ewv->ebrw",
            residual.astype(jnp.bfloat16),
            conv,
            preferred_element_type=jnp.float32,
        ).astype(jnp.bfloat16)
        grads = jnp.zeros((2 * group_tiles,) + observed.shape[1:], jnp.float32)
        for k in range(intersection_count):
            part = jnp.einsum(
                "ebrv,ewv->ebrw", back, matrices[:, k], preferred_element_type=jnp.float32
            )
            grads = grads + jnp.einsum(
                "et,ebrw->tbrw", onehots[:, k], part, precision=lax.Precision.HIGHEST
            )
        sky_out = sky_out + STEP * return_partials(grads, group_tiles)
    return (sky_out, residual)


def solution(mesh):
    in_specs = (
        P(("grp", "exp"), None, None, None),
        P(("grp", "exp"), None, None, None),
        P(("grp", "exp"), None),
        P(("grp", "exp"), None),
        P(("grp", "exp")),
        P(),
        P(),
        P(),
    )
    out_specs = (P(("grp", "exp"), None, None, None), P(("grp", "exp"), None, None, None))
    return jax.shard_map(shards, mesh=mesh, in_specs=in_specs, out_specs=out_specs, check_vma=False)
```

profile of v0, /device:TPU:0, one launch (start us, length us, event | category | flops | bytes accessed | tf_op | source)
XLA Modules:
  0.0 216.9 jit_solution(15102472466168929469)
XLA Ops:
  7.2 0.9 convert_element_type.69
  8.1 10.2 %all_gather.6 = bf16[4,6,8,512]{3,2,1,0:T(8,128)(2,1)S(1)} all-gather(bf16[1,6,8,512]{3,2,1,0:T(8,128)(2,1)S(1)} %convert_element_type.69), channel_id=1, replica_groups=mesh['grp'=8,'exp'=4] {'exp'}, dimensions={0}, use_global_device_ids=true | all-gather | bytes 245760 | tf_op jit(solution)/shard_map/all_gather | solution.py:31
  18.4 1.1 collective-permute-start
  19.5 0.8 copy.45
  20.3 10.1 %convolution_convert_fusion = bf16[4,4,512,512]{3,1,2,0:T(4,128)(2,1)} fusion(bf16[8,512,512]{2,1,0:T(8,128)(2,1)} %param.13, s32[4,4]{1,0:T(4,128)} %param.11), kind=kOutput, calls=%fused_computation | convolution fusion | flops 71303296 | bytes 12582976 | tf_op jit(solution)/shard_map/ekn,nwv->ekwv/dot_general | solution.py:68
  30.4 24.7 %fusion.107 = (bf16[4,1,512,512]{3,1,2,0:T(2,128)(2,1)S(1)}, bf16[4,1,512,512]{3,1,2,0:T(2,128)(2,1)S(1)}, bf16[4,1,512,512]{3,1,2,0:T(2,128)(2,1)S(1)}, bf16[4,1,512,512]{3,1,2,0:T(2,128)(2,1)S(1)}) fusion(bf16[4,4,512,512]{3,1,2,0:T(4,128)(2,1)} %convolution_convert_fusion), kind=kLoop, calls=%fused_computation.118 | loop fusion | bytes 16777216 | tf_op jit(solution)/shard_map/slice | solution.py:81
  55.7 1.9 copy.80
  57.6 1.9 copy.84
  59.5 2.0 copy.86
  62.2 2.6 %broadcast_in_dim.5 = bf16[4,512,1023]{2,1,0:T(8,128)(2,1)} broadcast(bf16[4,1023]{1,0:T(4,128)(2,1)S(1)} %maximum_convert_fusion), dimensions={0,2} | broadcast | bytes 4198392 | tf_op jit(solution)/shard_map/broadcast_in_dim | solution.py:23
  64.8 8.5 %reshape.61 = bf16[2095104]{0:T(1024)(128)(2,1)} reshape(bf16[4,512,1023]{2,1,0:T(8,128)(2,1)} %broadcast_in_dim.5) | data formatting | bytes 8380416
  73.3 5.8 %reshape.38 = bf16[4,523776]{1,0:T(4,128)(2,1)} reshape(bf16[2095104]{0:T(1024)(128)(2,1)} %reshape.61) | data formatting | bytes 8380416 | tf_op jit(solution)/shard_map/reshape | solution.py:23
  79.1 5.3 %slice.125 = bf16[4,523264]{1,0:T(4,128)(2,1)} slice(bf16[4,523776]{1,0:T(4,128)(2,1)} %reshape.38), slice={[0:4], [0:523264]} | slice | bytes 8372224 | tf_op jit(solution)/shard_map/slice | solution.py:26
  84.4 5.8 %reshape.63 = bf16[2093056]{0:T(1024)(128)(2,1)} reshape(bf16[4,523264]{1,0:T(4,128)(2,1)} %slice.125) | data formatting | bytes 8372224
  90.3 9.4 %reshape.39 = bf16[4,512,1022]{2,1,0:T(8,128)(2,1)} reshape(bf16[2093056]{0:T(1024)(128)(2,1)} %reshape.63) | data formatting | bytes 8372224 | tf_op jit(solution)/shard_map/reshape | solution.py:26
  100.2 1.7 fusion.109
  102.4 1.1 copy-done
  104.7 0.9 copy-done.7
  106.1 3.3 %convolution_convert_fusion.4 = bf16[4,6,8,512]{3,2,1,0:T(8,128)(2,1)S(1)} fusion(bf16[4,6,8,512]{3,2,1,0:T(8,128)(2,1)S(1)} %fusion.56, bf16[4,512,1022]{2,1,0:T(8,128)(2,1)} %reshape.39, bf16[4,6,8,512]{3,2,1,0:T(8,128)(2,1)S(1)} %copy-done.12), kind=kOutput, calls=%fused_computation.56 | convolution fusion | flops 201719808 | bytes 4775936 | tf_op jit(solution)/shard_map/ebrv,ewv->ebrw/dot_general | solution.py:87
  109.4 2.5 %fusion.30 = f32[4,6,8,512]{3,2,1,0:T(8,128)S(1)} fusion(bf16[4,6,8,512]{3,2,1,0:T(8,128)(2,1)S(1)} %convolution_convert_fusion.4, bf16[4,1,512,512]{3,2,1,0:T(8,128)(2,1)} %copy.80), kind=kOutput, calls=%fused_computation.32 | convolution fusion | flops 100663296 | bytes 2686976 | tf_op jit(solution)/shard_map/ebrv,ewv->ebrw/dot_general | solution.py:95
  111.9 0.7 fusion.22
  112.6 0.7 fusion.14
  113.5 0.7 fusion.6
  114.2 0.8 fusion.76
  115.0 0.8 convolution_add_fusion.5
  115.7 0.8 convolution_add_fusion.4
  116.5 0.8 convolution_add_fusion.3
  117.5 6.9 %collective-permute-done.1 = bf16[4,6,8,512]{3,0,2,1:T(4,128)(2,1)S(1)} collective-permute-done((bf16[4,6,8,512]{3,0,2,1:T(4,128)(2,1)S(1)}, bf16[4,6,8,512]{3,0,2,1:T(4,128)(2,1)S(1)}, u32[]{:S(2)}, u32[]{:S(2)}) %collective-permute-start.1) | collective-permute-done | bytes 196640 | tf_op jit(solution)/shard_map/ppermute | solution.py:13
  125.2 21.6 %reduce-scatter.7.cloned.1.call-done = bf16[1,6,8,512]{3,2,1,0:T(8,128)(2,1)} async-done(((bf16[4,6,8,512]{3,2,1,0:T(8,128)(2,1)}), bf16[1,6,8,512]{3,2,1,0:T(8,128)(2,1)}) %reduce-scatter.7.cloned.1.call-update) | async-done | bytes 49168
  146.8 0.8 fusion.97
  147.7 8.9 %all_gather.7 = bf16[4,6,8,512]{3,2,1,0:T(8,128)(2,1)S(1)} all-gather(bf16[1,6,8,512]{3,2,1,0:T(8,128)(2,1)S(1)} %fusion.97), channel_id=1, replica_groups=mesh['grp'=8,'exp'=4] {'exp'}, dimensions={0}, use_global_device_ids=true | all-gather | bytes 245760 | tf_op jit(solution)/shard_map/all_gather | solution.py:31
  157.2 3.2 %collective-permute-done.2 = bf16[4,6,8,512]{3,0,2,1:T(4,128)(2,1)S(1)} collective-permute-done((bf16[4,6,8,512]{3,0,2,1:T(4,128)(2,1)S(1)}, bf16[4,6,8,512]{3,0,2,1:T(4,128)(2,1)S(1)}, u32[]{:S(2)}, u32[]{:S(2)}) %collective-permute-start.2) | collective-permute-done | bytes 196640 | tf_op jit(solution)/shard_map/ppermute | solution.py:13
  160.8 1.4 fusion.108
  162.6 1.1 copy-done.1
  165.0 3.0 %convolution_subtract_fusion = f32[4,6,8,512]{3,2,1,0:T(8,128)S(1)} fusion(f32[4,6,8,512]{3,2,1,0:T(8,128)S(1)} %fusion.43, bf16[4,1,512,512]{3,2,1,0:T(8,128)(2,1)} %copy.86, bf16[4,512,1022]{2,1,0:T(8,128)(2,1)} %reshape.39, bf16[4,6,8,512]{3,2,1,0:T(8,128)(2,1)} %param.9, bf16[4,1,6,8,512]{4,1,3,2,0:T(2,128)(2,1)S(1)} %get-tuple-element.10), kind=kOutput, calls=%fused_computation.50 | convolution fusion | flops 201719808 | bytes 5373952 | tf_op jit(solution)/shard_map/ebrw,ewv->ebrv/dot_general | solution.py:83
  168.0 2.5 %convolution_convert_fusion.3 = bf16[4,6,8,512]{3,2,1,0:T(8,128)(2,1)S(1)} fusion(bf16[4,512,1022]{2,1,0:T(8,128)(2,1)} %reshape.39, f32[4,6,8,512]{3,2,1,0:T(8,128)S(1)} %convolution_subtract_fusion), kind=kOutput, calls=%fused_computation.55 | convolution fusion | flops 100859904 | bytes 2686976 | tf_op jit(solution)/shard_map/ebrv,ewv->ebrw/dot_general | solution.py:87
  170.5 2.3 %fusion.2 = f32[4,6,8,512]{3,2,1,0:T(8,128)S(1)} fusion(bf16[4,6,8,512]{3,2,1,0:T(8,128)(2,1)S(1)} %convolution_convert_fusion.3, bf16[4,1,512,512]{3,2,1,0:T(8,128)(2,1)} %copy.86), kind=kOutput, calls=%fused_computation.4 | convolution fusion | flops 100663296 | bytes 2686976 | tf_op jit(solution)/shard_map/ebrv,ewv->ebrw/dot_general | solution.py:95
  172.9 0.7 fusion.10
  173.6 0.7 fusion.18
  174.5 0.7 fusion.26
  175.2 0.8 fusion.71
  176.0 0.8 convolution_add_fusion.2
  176.7 0.8 convolution_add_fusion.1
  177.5 0.8 convolution_add_fusion
  178.4 1.7 collective-permute-start.3
  180.1 5.4 %collective-permute-done.3 = bf16[4,6,8,512]{3,0,2,1:T(4,128)(2,1)S(1)} collective-permute-done((bf16[4,6,8,512]{3,0,2,1:T(4,128)(2,1)S(1)}, bf16[4,6,8,512]{3,0,2,1:T(4,128)(2,1)S(1)}, u32[]{:S(2)}, u32[]{:S(2)}) %collective-permute-start.3) | collective-permute-done | bytes 196640 | tf_op jit(solution)/shard_map/ppermute | solution.py:13
  186.3 22.3 %reduce-scatter.9.cloned.1.call-done = bf16[1,6,8,512]{3,2,1,0:T(8,128)(2,1)} async-done(((bf16[4,6,8,512]{3,2,1,0:T(8,128)(2,1)}), bf16[1,6,8,512]{3,2,1,0:T(8,128)(2,1)}) %reduce-scatter.9.cloned.1.call-update) | async-done | bytes 49168
  208.6 1.5 multiply_add_fusion
  (64 shorter events, 9.0 us)
Async XLA Ops:
  7.2 139.7 %reduce-scatter.7.cloned.1.call-start = ((), (), s32[]{:S(2)}) async-start(), calls=%async_computation.2 | async-start | bytes 245760
  18.4 81.3 %collective-permute-start = (bf16[4,6,8,512]{3,0,2,1:T(4,128)(2,1)S(1)}, bf16[4,6,8,512]{3,0,2,1:T(4,128)(2,1)S(1)}, u32[]{:S(2)}, u32[]{:S(2)}) collective-permute-start(bf16[4,6,8,512]{3,0,2,1:T(4,128)(2,1)S(1)} %copy.47), channel_id=1, source_target_pairs={{4,0},{8,4},{12,8},{16,12},{20,16},{24,20},{28,24},{0,28},{5,1},{9... | collective-permute-start | bytes 589832 | tf_op jit(solution)/shard_map/ppermute | solution.py:13
  59.5 2.0 copy-start.15
  59.5 2.0 copy-start.14
  59.5 2.1 copy-start.13
  101.9 1.6 copy-start
  102.4 1.9 copy-start.3
  104.0 1.7 copy-start.7
  104.7 1.4 copy-start.12
  109.4 3.2 %copy-start.4 = (bf16[4,1,512,512]{3,2,1,0:T(8,128)(2,1)S(1)}, bf16[4,1,512,512]{3,2,1,0:T(8,128)(2,1)}, u32[]{:S(2)}) copy-start(bf16[4,1,512,512]{3,2,1,0:T(8,128)(2,1)} %copy.84) | copy-start | bytes 6291460
  111.9 1.6 copy-start.8
  116.5 30.3 %copy-start.10 = (f32[1,6,8,512]{3,2,1,0:T(8,128)S(1)}, f32[1,6,8,512]{3,2,1,0:T(8,128)}, u32[]{:S(2)}) copy-start(f32[1,6,8,512]{3,2,1,0:T(8,128)} %param.8) | copy-start | bytes 294916
  117.4 6.9 %collective-permute-start.1 = (bf16[4,6,8,512]{3,0,2,1:T(4,128)(2,1)S(1)}, bf16[4,6,8,512]{3,0,2,1:T(4,128)(2,1)S(1)}, u32[]{:S(2)}, u32[]{:S(2)}) collective-permute-start(bf16[4,6,8,512]{3,0,2,1:T(4,128)(2,1)S(1)} %slice.164), channel_id=1, source_target_pairs={{28,0},{0,4},{4,8},{8,12},{12,16},{16,20},{20,24},{24,28},{29,1},{... | collective-permute-start | bytes 589832 | tf_op jit(solution)/shard_map/ppermute | solution.py:13
  125.2 83.4 %reduce-scatter.9.cloned.1.call-start = ((), (), s32[]{:S(2)}) async-start(), calls=%async_computation.3 | async-start | bytes 245760
  156.7 3.6 %collective-permute-start.2 = (bf16[4,6,8,512]{3,0,2,1:T(4,128)(2,1)S(1)}, bf16[4,6,8,512]{3,0,2,1:T(4,128)(2,1)S(1)}, u32[]{:S(2)}, u32[]{:S(2)}) collective-permute-start(bf16[4,6,8,512]{3,0,2,1:T(4,128)(2,1)S(1)} %copy.56), channel_id=1, source_target_pairs={{4,0},{8,4},{12,8},{16,12},{20,16},{24,20},{28,24},{0,28},{5,1},{9... | collective-permute-start | bytes 589832 | tf_op jit(solution)/shard_map/ppermute | solution.py:13
  162.2 1.6 copy-start.1
  162.6 1.9 copy-start.5
  168.0 4.8 %copy-start.9 = (f32[4,6,8,512]{3,2,1,0:T(8,128)}, f32[4,6,8,512]{3,2,1,0:T(8,128)S(1)}, u32[]{:S(2)}) copy-start(f32[4,6,8,512]{3,2,1,0:T(8,128)S(1)} %convolution_subtract_fusion) | copy-start | bytes 1179652
  168.0 4.8 %copy-start.6 = (bf16[4,1,512,512]{3,2,1,0:T(8,128)(2,1)S(1)}, bf16[4,1,512,512]{3,2,1,0:T(8,128)(2,1)}, u32[]{:S(2)}) copy-start(bf16[4,1,512,512]{3,2,1,0:T(8,128)(2,1)} %copy.84) | copy-start | bytes 6291460
  172.9 1.6 copy-start.2
  177.5 31.1 %copy-start.11 = (bf16[1,6,8,512]{3,2,1,0:T(8,128)(2,1)S(1)}, bf16[1,6,8,512]{3,2,1,0:T(8,128)(2,1)}, u32[]{:S(2)}) copy-start(bf16[1,6,8,512]{3,2,1,0:T(8,128)(2,1)} %reduce-scatter.7.cloned.1.call-done) | copy-start | bytes 147460
  178.4 7.1 %collective-permute-start.3 = (bf16[4,6,8,512]{3,0,2,1:T(4,128)(2,1)S(1)}, bf16[4,6,8,512]{3,0,2,1:T(4,128)(2,1)S(1)}, u32[]{:S(2)}, u32[]{:S(2)}) collective-permute-start(bf16[4,6,8,512]{3,0,2,1:T(4,128)(2,1)S(1)} %slice.163), channel_id=1, source_target_pairs={{28,0},{0,4},{4,8},{8,12},{12,16},{16,20},{20,24},{24,28},{29,1},{... | collective-permute-start | bytes 589832 | tf_op jit(solution)/shard_map/ppermute | solution.py:13
Sparse Core Ops, SparseCore 0:
  125.3 21.4 reduce-scatter.6
  186.5 22.0 reduce-scatter.8
where the time goes:
time: 218 us; the launch traced here: 217 us
  local copies, waits for them, and re-layouts  78.7 us (36%)
  waiting for transfers between devices  59.4 us (27%)
  matrix products  38.2 us (18%)
  blocking collectives  19.1 us (9%)
  between operations  14.5 us (7%)
  other arithmetic  3.8 us (2%)
  starting transfers between devices  3.34 us (2%)
    unnamed x4, waiting for transfers between devices  43.9 us
    unnamed x39, local copies, waits for them, and re-layouts  25.5 us
    slice x1, local copies, waits for them, and re-layouts, shards(): matrices[:, k]  24.7 us
    all_gather x2, blocking collectives, fetch_window(): own_group = lax.all_gather(sky_half, 'exp', axis=0, tiled=True)  19.1 us
    ppermute x4, waiting for transfers between devices, shifted(): return lax.ppermute(block, axis, route)  15.5 us
    dot_general x1, matrix products, shards(): jnp.einsum('ekn,nwv->ekwv', pick_res, resample_table, preferred_element_t...  10.1 us
    reshape x1, local copies, waits for them, and re-layouts, conv_matrices(): tiled[:, :width * (2 * width - 2)].reshape(count, width, 2 * width - 2)  9.37 us
    dot_general x8, matrix products, shards(): jnp.einsum('ebrv,ewv->ebrw', back, matrices[:, k], preferred_element_type...  9.1 us
  transfers between devices with their start and end apart: 6, of which 5 were waited for; matrix products, arithmetic and copies ran while one was open for 37% of the time, Pallas kernels for 0%

commit v1 on v0

--- a/solution.py
+++ b/solution.py
@@ -5,6 +5,12 @@
 
 ITERS = 2
 STEP = 0.05
+
+
+def joined_along(tiles, dim):
+    shape = list(tiles.shape[1:])
+    shape[dim] *= tiles.shape[0]
+    return jnp.moveaxis(tiles, 0, dim).reshape(shape)
 
 
 def shifted(block, axis, distance):
@@ -28,7 +34,19 @@
 
 
 def fetch_window(sky_half):
-    own_group = lax.all_gather(sky_half, "exp", axis=0, tiled=True)
+    peers = lax.axis_size("exp")
+    pairs = [(i_2, (i_2 + 1) % peers) for i_2 in range(peers)]
+    back_2 = [(b, a) for a, b in pairs]
+    lower, upper = ([], [])
+    for step_2 in range(peers - 1):
+        if step_2 % 2 == 0:
+            lower.append(lax.ppermute(lower[-1] if lower else sky_half, "exp", pairs))
+        else:
+            upper.append(lax.ppermute(upper[-1] if upper else sky_half, "exp", back_2))
+    tiles = jnp.stack([*lower[::-1], sky_half, *upper])
+    shift = lax.axis_index("exp") - len(lower)
+    tiles = tiles[(jnp.arange(peers) - shift) % peers]
+    own_group = joined_along(tiles, 0)
     next_group = shifted(own_group, "grp", -1)
     return jnp.concatenate([own_group, next_group], axis=0)
 

time: 218 us -> 227 us (1.041)
  blocking collectives: 19.1 us -> 0 us
  waiting for transfers between devices: 59.4 us -> 69.7 us
  starting transfers between devices: 3.34 us -> 13.6 us
  local copies, waits for them, and re-layouts: 78.7 us -> 85.4 us
    all_gather x2 -> x0, blocking collectives: 19.1 us -> none  [fetch_window(): own_group = lax.all_gather(sky_half, 'exp', axis=0, tiled=True)]
    ppermute x0 -> x6, starting transfers between devices: none -> 8.83 us  [the longest x4 6.3 us: fetch_window(): lower.append(lax.ppermute(lower[-1] if lower else sky_half, 'exp', pairs))]
    ppermute x0 -> x6, waiting for transfers between devices: none -> 6.4 us  [the longest x4 6.39 us: fetch_window(): lower.append(lax.ppermute(lower[-1] if lower else sky_half, 'exp', pairs))]
    unnamed x39 -> x47, local copies, waits for them, and re-layouts: 25.5 us -> 29.6 us
    ppermute x4, waiting for transfers between devices: 15.5 us -> 18.7 us  [shifted(): return lax.ppermute(block, axis, route)]
  transfers between devices with their start and end apart: 6 -> 12, of which waited for: 5 -> 8; matrix products, arithmetic and copies ran while one was open for 37% -> 37% of each run, Pallas kernels for 0% -> 0%
where the time goes in v1:
time: 227 us; the launch traced here: 226 us
  local copies, waits for them, and re-layouts  85.4 us (38%)
  waiting for transfers between devices  69.7 us (31%)
  matrix products  38.3 us (17%)
  between operations  14.5 us (6%)
  starting transfers between devices  13.6 us (6%)
  other arithmetic  4.77 us (2%)
    unnamed x4, waiting for transfers between devices  44.6 us
    unnamed x47, local copies, waits for them, and re-layouts  29.6 us
    slice x1, local copies, waits for them, and re-layouts, shards(): matrices[:, k]  26.6 us
    ppermute x4, waiting for transfers between devices, shifted(): return lax.ppermute(block, axis, route)  18.7 us
    dot_general x1, matrix products, shards(): jnp.einsum('ekn,nwv->ekwv', pick_res, resample_table, preferred_element_t...  10.2 us
    reshape x1, local copies, waits for them, and re-layouts, conv_matrices(): tiled[:, :width * (2 * width - 2)].reshape(count, width, 2 * width - 2)  9.34 us
    dot_general x8, matrix products, shards(): jnp.einsum('ebrv,ewv->ebrw', back, matrices[:, k], preferred_element_type...  9.1 us
    ppermute x4, waiting for transfers between devices, fetch_window(): lower.append(lax.ppermute(lower[-1] if lower else sky_half, 'exp', pairs))  6.39 us
  transfers between devices with their start and end apart: 12, of which 8 were waited for; matrix products, arithmetic and copies ran while one was open for 37% of the time, Pallas kernels for 0%

profile of v1, /device:TPU:0, one launch (start us, length us, event | category | flops | bytes accessed | tf_op | source)
XLA Modules:
  0.0 226.2 jit_solution(9839091625931382023)
XLA Ops:
  7.2 0.9 convert_element_type.69
  8.1 2.9 %collective-permute-start = (bf16[1,6,8,512]{3,2,1,0:T(8,128)(2,1)S(1)}, bf16[1,6,8,512]{3,2,1,0:T(8,128)(2,1)S(1)}, u32[]{:S(2)}, u32[]{:S(2)}) collective-permute-start(bf16[1,6,8,512]{3,2,1,0:T(8,128)(2,1)S(1)} %convert_element_type.69), channel_id=1, source_target_pairs={{0,1},{1,2},{2,3},{3,0},{4,5},{5,6},{6,7},{7,4},{8,9},{9,10},{10,1... | collective-permute-start | bytes 147464 | tf_op jit(solution)/shard_map/ppermute | solution.py:43
  11.1 1.0 collective-permute-start.2
  12.1 0.9 convert_bitcast_fusion
  13.0 10.2 %convolution_convert_fusion = bf16[4,4,512,512]{3,1,2,0:T(4,128)(2,1)} fusion(bf16[8,512,512]{2,1,0:T(8,128)(2,1)} %param.13, s32[4,4]{1,0:T(4,128)} %param.11), kind=kOutput, calls=%fused_computation.2 | convolution fusion | flops 71303296 | bytes 12582976 | tf_op jit(solution)/shard_map/ekn,nwv->ekwv/dot_general | solution.py:86
  23.1 26.6 %fusion.109 = (bf16[4,1,512,512]{3,1,2,0:T(2,128)(2,1)}, bf16[4,1,512,512]{3,1,2,0:T(2,128)(2,1)}, bf16[4,1,512,512]{3,1,2,0:T(2,128)(2,1)}, bf16[4,1,512,512]{3,1,2,0:T(2,128)(2,1)}) fusion(bf16[4,4,512,512]{3,1,2,0:T(4,128)(2,1)} %convolution_convert_fusion), kind=kLoop, calls=%fused_computation.129 | loop fusion | bytes 16777216 | tf_op jit(solution)/shard_map/slice | solution.py:99
  50.5 1.2 collective-permute-start.1
  51.9 3.0 %copy.170 = bf16[4,1,512,512]{3,2,1,0:T(8,128)(2,1)S(1)} copy(bf16[4,1,512,512]{3,1,2,0:T(2,128)(2,1)} %get-tuple-element.14) | data formatting | bytes 4194304
  55.3 2.0 copy.168
  57.3 1.0 copy-done.10
  58.2 1.9 copy.172
  60.2 1.0 copy-done.9
  61.2 1.9 copy.174
  63.1 2.5 %broadcast_in_dim.5 = bf16[4,512,1023]{2,1,0:T(8,128)(2,1)} broadcast(bf16[4,1023]{1,0:T(4,128)(2,1)S(1)} %maximum_convert_fusion), dimensions={0,2} | broadcast | bytes 4198392 | tf_op jit(solution)/shard_map/broadcast_in_dim | solution.py:29
  65.6 8.6 %reshape.140 = bf16[2095104]{0:T(1024)(128)(2,1)} reshape(bf16[4,512,1023]{2,1,0:T(8,128)(2,1)} %broadcast_in_dim.5) | data formatting | bytes 8380416
  74.1 5.7 %reshape.94 = bf16[4,523776]{1,0:T(4,128)(2,1)} reshape(bf16[2095104]{0:T(1024)(128)(2,1)} %reshape.140) | data formatting | bytes 8380416 | tf_op jit(solution)/shard_map/reshape | solution.py:29
  79.8 5.4 %slice.129 = bf16[4,523264]{1,0:T(4,128)(2,1)} slice(bf16[4,523776]{1,0:T(4,128)(2,1)} %reshape.94), slice={[0:4], [0:523264]} | slice | bytes 8372224 | tf_op jit(solution)/shard_map/slice | solution.py:32
  85.2 5.7 %reshape.142 = bf16[2093056]{0:T(1024)(128)(2,1)} reshape(bf16[4,523264]{1,0:T(4,128)(2,1)} %slice.129) | data formatting | bytes 8372224
  90.9 9.3 %reshape.95 = bf16[4,512,1022]{2,1,0:T(8,128)(2,1)} reshape(bf16[2093056]{0:T(1024)(128)(2,1)} %reshape.142) | data formatting | bytes 8372224 | tf_op jit(solution)/shard_map/reshape | solution.py:32
  101.0 2.5 %collective-permute-start.3 = (bf16[4,6,8,512]{3,0,2,1:T(4,128)(2,1)S(1)}, bf16[4,6,8,512]{3,0,2,1:T(4,128)(2,1)S(1)}, u32[]{:S(2)}, u32[]{:S(2)}) collective-permute-start(bf16[4,6,8,512]{3,0,2,1:T(4,128)(2,1)S(1)} %copy.131), channel_id=1, source_target_pairs={{4,0},{8,4},{12,8},{16,12},{20,16},{24,20},{28,24},{0,28},{5,1},{9... | collective-permute-start | bytes 589832 | tf_op jit(solution)/shard_map/ppermute | solution.py:19
  103.6 3.1 %collective-permute-done.3 = bf16[4,6,8,512]{3,0,2,1:T(4,128)(2,1)S(1)} collective-permute-done((bf16[4,6,8,512]{3,0,2,1:T(4,128)(2,1)S(1)}, bf16[4,6,8,512]{3,0,2,1:T(4,128)(2,1)S(1)}, u32[]{:S(2)}, u32[]{:S(2)}) %collective-permute-start.3) | collective-permute-done | bytes 196640 | tf_op jit(solution)/shard_map/ppermute | solution.py:19
  107.1 1.7 fusion.111
  109.3 1.1 copy-done
  111.7 0.9 copy-done.7
  113.0 3.4 %convolution_convert_fusion.4 = bf16[4,6,8,512]{3,2,1,0:T(8,128)(2,1)S(1)} fusion(bf16[4,6,8,512]{3,2,1,0:T(8,128)(2,1)S(1)} %fusion.56, bf16[4,512,1022]{2,1,0:T(8,128)(2,1)} %reshape.95, bf16[4,6,8,512]{3,2,1,0:T(8,128)(2,1)S(1)} %copy-done.15), kind=kOutput, calls=%fused_computation.58 | convolution fusion | flops 201719808 | bytes 4775936 | tf_op jit(solution)/shard_map/ebrv,ewv->ebrw/dot_general | solution.py:105
  116.4 2.5 %fusion.30 = f32[4,6,8,512]{3,2,1,0:T(8,128)S(1)} fusion(bf16[4,6,8,512]{3,2,1,0:T(8,128)(2,1)S(1)} %convolution_convert_fusion.4, bf16[4,1,512,512]{3,2,1,0:T(8,128)(2,1)} %copy.168), kind=kOutput, calls=%fused_computation.34 | convolution fusion | flops 100663296 | bytes 2686976 | tf_op jit(solution)/shard_map/ebrv,ewv->ebrw/dot_general | solution.py:113
  122.0 0.8 convolution_add_fusion.5
  122.7 0.8 convolution_add_fusion.4
  123.5 0.8 convolution_add_fusion.3
  124.5 7.1 %collective-permute-done.4 = bf16[4,6,8,512]{3,0,2,1:T(4,128)(2,1)S(1)} collective-permute-done((bf16[4,6,8,512]{3,0,2,1:T(4,128)(2,1)S(1)}, bf16[4,6,8,512]{3,0,2,1:T(4,128)(2,1)S(1)}, u32[]{:S(2)}, u32[]{:S(2)}) %collective-permute-start.4) | collective-permute-done | bytes 196640 | tf_op jit(solution)/shard_map/ppermute | solution.py:19
  132.4 22.3 %reduce-scatter.7.cloned.1.call-done = bf16[1,6,8,512]{3,2,1,0:T(8,128)(2,1)} async-done(((bf16[4,6,8,512]{3,2,1,0:T(8,128)(2,1)}), bf16[1,6,8,512]{3,2,1,0:T(8,128)(2,1)}) %reduce-scatter.7.cloned.1.call-update) | async-done | bytes 49168
  154.7 0.8 fusion.97
  155.5 1.5 collective-permute-start.5
  157.0 1.5 collective-permute-start.7
  158.5 2.1 collective-permute-done.5
  161.2 4.3 %collective-permute-done.6 = bf16[1,6,8,512]{3,2,1,0:T(8,128)(2,1)S(1)} collective-permute-done((bf16[1,6,8,512]{3,2,1,0:T(8,128)(2,1)S(1)}, bf16[1,6,8,512]{3,2,1,0:T(8,128)(2,1)S(1)}, u32[]{:S(2)}, u32[]{:S(2)}) %collective-permute-start.6) | collective-permute-done | bytes 49184 | tf_op jit(solution)/shard_map/ppermute | solution.py:43
  166.6 3.2 %collective-permute-done.8 = bf16[4,6,8,512]{3,0,2,1:T(4,128)(2,1)S(1)} collective-permute-done((bf16[4,6,8,512]{3,0,2,1:T(4,128)(2,1)S(1)}, bf16[4,6,8,512]{3,0,2,1:T(4,128)(2,1)S(1)}, u32[]{:S(2)}, u32[]{:S(2)}) %collective-permute-start.8) | collective-permute-done | bytes 196640 | tf_op jit(solution)/shard_map/ppermute | solution.py:19
  170.2 1.1 fusion.110
  171.9 1.1 copy-done.1
  174.2 3.0 %convolution_subtract_fusion = f32[4,6,8,512]{3,2,1,0:T(8,128)S(1)} fusion(f32[4,6,8,512]{3,2,1,0:T(8,128)S(1)} %fusion.43, bf16[4,1,512,512]{3,2,1,0:T(8,128)(2,1)} %copy.174, bf16[4,512,1022]{2,1,0:T(8,128)(2,1)} %reshape.95, bf16[4,6,8,512]{3,2,1,0:T(8,128)(2,1)} %param.9, bf16[4,1,6,8,512]{4,1,3,2,0:T(2,128)(2,1)S(1)} %get-tuple-element.16), kind=kOutput, calls=%fused_computation.52 | convolution fusion | flops 201719808 | bytes 5373952 | tf_op jit(solution)/shard_map/ebrw,ewv->ebrv/dot_general | solution.py:101
  177.3 2.5 %convolution_convert_fusion.3 = bf16[4,6,8,512]{3,2,1,0:T(8,128)(2,1)S(1)} fusion(bf16[4,512,1022]{2,1,0:T(8,128)(2,1)} %reshape.95, f32[4,6,8,512]{3,2,1,0:T(8,128)S(1)} %convolution_subtract_fusion), kind=kOutput, calls=%fused_computation.57 | convolution fusion | flops 100859904 | bytes 2686976 | tf_op jit(solution)/shard_map/ebrv,ewv->ebrw/dot_general | solution.py:105
  179.8 2.3 %fusion.2 = f32[4,6,8,512]{3,2,1,0:T(8,128)S(1)} fusion(bf16[4,6,8,512]{3,2,1,0:T(8,128)(2,1)S(1)} %convolution_convert_fusion.3, bf16[4,1,512,512]{3,2,1,0:T(8,128)(2,1)} %copy.174), kind=kOutput, calls=%fused_computation.6 | convolution fusion | flops 100663296 | bytes 2686976 | tf_op jit(solution)/shard_map/ebrv,ewv->ebrw/dot_general | solution.py:113
  185.2 0.8 convolution_add_fusion.2
  186.0 0.8 convolution_add_fusion.1
  187.6 1.8 collective-permute-start.9
  189.4 5.3 %collective-permute-done.9 = bf16[4,6,8,512]{3,0,2,1:T(4,128)(2,1)S(1)} collective-permute-done((bf16[4,6,8,512]{3,0,2,1:T(4,128)(2,1)S(1)}, bf16[4,6,8,512]{3,0,2,1:T(4,128)(2,1)S(1)}, u32[]{:S(2)}, u32[]{:S(2)}) %collective-permute-start.9) | collective-permute-done | bytes 196640 | tf_op jit(solution)/shard_map/ppermute | solution.py:19
  195.6 22.3 %reduce-scatter.9.cloned.1.call-done = bf16[1,6,8,512]{3,2,1,0:T(8,128)(2,1)} async-done(((bf16[4,6,8,512]{3,2,1,0:T(8,128)(2,1)}), bf16[1,6,8,512]{3,2,1,0:T(8,128)(2,1)}) %reduce-scatter.9.cloned.1.call-update) | async-done | bytes 49168
  217.9 1.5 multiply_add_fusion
  (89 shorter events, 17.3 us)
Async XLA Ops:
  7.2 147.5 %reduce-scatter.7.cloned.1.call-start = ((), (), s32[]{:S(2)}) async-start(), calls=%async_computation.2 | async-start | bytes 245760
  8.1 42.4 %collective-permute-start = (bf16[1,6,8,512]{3,2,1,0:T(8,128)(2,1)S(1)}, bf16[1,6,8,512]{3,2,1,0:T(8,128)(2,1)S(1)}, u32[]{:S(2)}, u32[]{:S(2)}) collective-permute-start(bf16[1,6,8,512]{3,2,1,0:T(8,128)(2,1)S(1)} %convert_element_type.69), channel_id=1, source_target_pairs={{0,1},{1,2},{2,3},{3,0},{4,5},{5,6},{6,7},{7,4},{8,9},{9,10},{10,1... | collective-permute-start | bytes 147464 | tf_op jit(solution)/shard_map/ppermute | solution.py:43
  11.1 89.2 %collective-permute-start.2 = (bf16[1,6,8,512]{3,2,1,0:T(8,128)(2,1)S(1)}, bf16[1,6,8,512]{3,2,1,0:T(8,128)(2,1)S(1)}, u32[]{:S(2)}, u32[]{:S(2)}) collective-permute-start(bf16[1,6,8,512]{3,2,1,0:T(8,128)(2,1)S(1)} %convert_element_type.69), channel_id=1, source_target_pairs={{1,0},{2,1},{3,2},{0,3},{5,4},{6,5},{7,6},{4,7},{9,8},{10,9},{11,1... | collective-permute-start | bytes 147464 | tf_op jit(solution)/shard_map/ppermute | solution.py:45
  23.1 26.7 %copy-start.19 = (s32[4]{0:T(128)S(1)}, s32[4]{0:T(128)}, u32[]{:S(2)}) copy-start(s32[4]{0:T(128)} %param.12) | copy-start | bytes 52
  23.1 26.7 %copy-start.17 = (f32[16,8]{0,1:T(8,128)S(1)}, f32[16,8]{0,1:T(8,128)}, u32[]{:S(2)}) copy-start(f32[16,8]{0,1:T(8,128)} %param.14) | copy-start | bytes 1540
  23.1 26.8 %copy-start.16 = (f32[8,41]{1,0:T(8,128)S(1)}, f32[8,41]{1,0:T(8,128)}, u32[]{:S(2)}) copy-start(f32[8,41]{1,0:T(8,128)} %param.15) | copy-start | bytes 3940
  23.1 28.6 %copy-start.18 = (s32[4,4]{1,0:T(4,128)S(1)}, s32[4,4]{1,0:T(4,128)}, u32[]{:S(2)}) copy-start(s32[4,4]{1,0:T(4,128)} %param.10) | copy-start | bytes 196
  50.5 49.8 %collective-permute-start.1 = (bf16[1,6,8,512]{3,2,1,0:T(8,128)(2,1)S(1)}, bf16[1,6,8,512]{3,2,1,0:T(8,128)(2,1)S(1)}, u32[]{:S(2)}, u32[]{:S(2)}) collective-permute-start(bf16[1,6,8,512]{3,2,1,0:T(8,128)(2,1)S(1)} %collective-permute-done), channel_id=1, source_target_pairs={{0,1},{1,2},{2,3},{3,0},{4,5},{5,6},{6,7},{7,4},{8,9},{9,10},{10,1... | collective-permute-start | bytes 147464 | tf_op jit(solution)/shard_map/ppermute | solution.py:43
  51.8 3.4 %copy-start.11 = (bf16[4,1,512,512]{3,1,2,0:T(2,128)(2,1)S(1)}, bf16[4,1,512,512]{3,1,2,0:T(2,128)(2,1)}, u32[]{:S(2)}) copy-start(bf16[4,1,512,512]{3,1,2,0:T(2,128)(2,1)} %get-tuple-element.15) | copy-start | bytes 6291460
  55.3 2.9 %copy-start.10 = (bf16[4,1,512,512]{3,1,2,0:T(2,128)(2,1)S(1)}, bf16[4,1,512,512]{3,1,2,0:T(2,128)(2,1)}, u32[]{:S(2)}) copy-start(bf16[4,1,512,512]{3,1,2,0:T(2,128)(2,1)} %get-tuple-element.13) | copy-start | bytes 6291460
  58.2 2.9 %copy-start.9 = (bf16[4,1,512,512]{3,1,2,0:T(2,128)(2,1)S(1)}, bf16[4,1,512,512]{3,1,2,0:T(2,128)(2,1)}, u32[]{:S(2)}) copy-start(bf16[4,1,512,512]{3,1,2,0:T(2,128)(2,1)} %get-tuple-element.12) | copy-start | bytes 6291460
  101.0 5.7 %collective-permute-start.3 = (bf16[4,6,8,512]{3,0,2,1:T(4,128)(2,1)S(1)}, bf16[4,6,8,512]{3,0,2,1:T(4,128)(2,1)S(1)}, u32[]{:S(2)}, u32[]{:S(2)}) collective-permute-start(bf16[4,6,8,512]{3,0,2,1:T(4,128)(2,1)S(1)} %copy.131), channel_id=1, source_target_pairs={{4,0},{8,4},{12,8},{16,12},{20,16},{24,20},{28,24},{0,28},{5,1},{9... | collective-permute-start | bytes 589832 | tf_op jit(solution)/shard_map/ppermute | solution.py:19
  108.9 1.6 copy-start
  109.3 1.9 copy-start.3
  110.9 1.7 copy-start.7
  111.7 1.4 copy-start.15
  116.4 3.2 %copy-start.4 = (bf16[4,1,512,512]{3,2,1,0:T(8,128)(2,1)S(1)}, bf16[4,1,512,512]{3,2,1,0:T(8,128)(2,1)}, u32[]{:S(2)}) copy-start(bf16[4,1,512,512]{3,2,1,0:T(8,128)(2,1)} %copy.172) | copy-start | bytes 6291460
  118.9 1.6 copy-start.8
  123.5 31.2 %copy-start.12 = (f32[1,6,8,512]{3,2,1,0:T(8,128)S(1)}, f32[1,6,8,512]{3,2,1,0:T(8,128)}, u32[]{:S(2)}) copy-start(f32[1,6,8,512]{3,2,1,0:T(8,128)} %param.8) | copy-start | bytes 294916
  124.4 7.1 %collective-permute-start.4 = (bf16[4,6,8,512]{3,0,2,1:T(4,128)(2,1)S(1)}, bf16[4,6,8,512]{3,0,2,1:T(4,128)(2,1)S(1)}, u32[]{:S(2)}, u32[]{:S(2)}) collective-permute-start(bf16[4,6,8,512]{3,0,2,1:T(4,128)(2,1)S(1)} %slice.168), channel_id=1, source_target_pairs={{28,0},{0,4},{4,8},{8,12},{12,16},{16,20},{20,24},{24,28},{29,1},{... | collective-permute-start | bytes 589832 | tf_op jit(solution)/shard_map/ppermute | solution.py:19
  132.4 85.5 %reduce-scatter.9.cloned.1.call-start = ((), (), s32[]{:S(2)}) async-start(), calls=%async_computation.3 | async-start | bytes 245760
  155.5 5.0 %collective-permute-start.5 = (bf16[1,6,8,512]{3,2,1,0:T(8,128)(2,1)S(1)}, bf16[1,6,8,512]{3,2,1,0:T(8,128)(2,1)S(1)}, u32[]{:S(2)}, u32[]{:S(2)}) collective-permute-start(bf16[1,6,8,512]{3,2,1,0:T(8,128)(2,1)S(1)} %fusion.97), channel_id=1, source_target_pairs={{0,1},{1,2},{2,3},{3,0},{4,5},{5,6},{6,7},{7,4},{8,9},{9,10},{10,1... | collective-permute-start | bytes 147464 | tf_op jit(solution)/shard_map/ppermute | solution.py:43
  157.0 4.2 %collective-permute-start.7 = (bf16[1,6,8,512]{3,2,1,0:T(8,128)(2,1)S(1)}, bf16[1,6,8,512]{3,2,1,0:T(8,128)(2,1)S(1)}, u32[]{:S(2)}, u32[]{:S(2)}) collective-permute-start(bf16[1,6,8,512]{3,2,1,0:T(8,128)(2,1)S(1)} %fusion.97), channel_id=1, source_target_pairs={{1,0},{2,1},{3,2},{0,3},{5,4},{6,5},{7,6},{4,7},{9,8},{10,9},{11,1... | collective-permute-start | bytes 147464 | tf_op jit(solution)/shard_map/ppermute | solution.py:45
  160.6 5.0 %collective-permute-start.6 = (bf16[1,6,8,512]{3,2,1,0:T(8,128)(2,1)S(1)}, bf16[1,6,8,512]{3,2,1,0:T(8,128)(2,1)S(1)}, u32[]{:S(2)}, u32[]{:S(2)}) collective-permute-start(bf16[1,6,8,512]{3,2,1,0:T(8,128)(2,1)S(1)} %collective-permute-done.5), channel_id=1, source_target_pairs={{0,1},{1,2},{2,3},{3,0},{4,5},{5,6},{6,7},{7,4},{8,9},{9,10},{10,1... | collective-permute-start | bytes 147464 | tf_op jit(solution)/shard_map/ppermute | solution.py:43
  166.3 3.5 %collective-permute-start.8 = (bf16[4,6,8,512]{3,0,2,1:T(4,128)(2,1)S(1)}, bf16[4,6,8,512]{3,0,2,1:T(4,128)(2,1)S(1)}, u32[]{:S(2)}, u32[]{:S(2)}) collective-permute-start(bf16[4,6,8,512]{3,0,2,1:T(4,128)(2,1)S(1)} %copy.144), channel_id=1, source_target_pairs={{4,0},{8,4},{12,8},{16,12},{20,16},{24,20},{28,24},{0,28},{5,1},{9... | collective-permute-start | bytes 589832 | tf_op jit(solution)/shard_map/ppermute | solution.py:19
  171.4 1.6 copy-start.1
  171.9 1.9 copy-start.5
  177.2 4.8 %copy-start.13 = (f32[4,6,8,512]{3,2,1,0:T(8,128)}, f32[4,6,8,512]{3,2,1,0:T(8,128)S(1)}, u32[]{:S(2)}) copy-start(f32[4,6,8,512]{3,2,1,0:T(8,128)S(1)} %convolution_subtract_fusion) | copy-start | bytes 1179652
  177.2 4.8 %copy-start.6 = (bf16[4,1,512,512]{3,2,1,0:T(8,128)(2,1)S(1)}, bf16[4,1,512,512]{3,2,1,0:T(8,128)(2,1)}, u32[]{:S(2)}) copy-start(bf16[4,1,512,512]{3,2,1,0:T(8,128)(2,1)} %copy.172) | copy-start | bytes 6291460
  182.1 1.6 copy-start.2
  186.7 31.2 %copy-start.14 = (bf16[1,6,8,512]{3,2,1,0:T(8,128)(2,1)S(1)}, bf16[1,6,8,512]{3,2,1,0:T(8,128)(2,1)}, u32[]{:S(2)}) copy-start(bf16[1,6,8,512]{3,2,1,0:T(8,128)(2,1)} %reduce-scatter.7.cloned.1.call-done) | copy-start | bytes 147460
  187.6 7.1 %collective-permute-start.9 = (bf16[4,6,8,512]{3,0,2,1:T(4,128)(2,1)S(1)}, bf16[4,6,8,512]{3,0,2,1:T(4,128)(2,1)S(1)}, u32[]{:S(2)}, u32[]{:S(2)}) collective-permute-start(bf16[4,6,8,512]{3,0,2,1:T(4,128)(2,1)S(1)} %slice.167), channel_id=1, source_target_pairs={{28,0},{0,4},{4,8},{8,12},{12,16},{16,20},{20,24},{24,28},{29,1},{... | collective-permute-start | bytes 589832 | tf_op jit(solution)/shard_map/ppermute | solution.py:19
Sparse Core Ops, SparseCore 0:
  132.5 22.1 reduce-scatter.6
  195.7 22.1 reduce-scatter.8
